TPU v7x, 256 devices: a whole 4x4x8 slice. The times are simulated.
256 devices in a mesh: rep: 2 (over core), src: 16 (over z_lo, x), tgt: 8 (over z_hi, y).
Axes of the slice: x: 4, y: 4, z: 8 (z_hi: 2, z_lo: 4; z = z_hi * 4 + z_lo), core: 2. Of those that a mesh axis runs over, the one named last changes fastest.
Arguments:
- src_feats: float32 [2, 2048, 3200], P('rep', ('src', 'tgt')), may hold values from -6 to 6
- tgt_cotangent: float32 [2, 2048, 3200], P('rep', ('tgt', 'src')), may hold values from -0.6 to 0.6
- rotation: float32 [2, 16, 8, 115, 384], P('rep', 'src', 'tgt'), may hold values from -3 to 3
- edge_src: int32 [2, 16, 8, 384], P('rep', 'src', 'tgt'), may hold values from 0 to 127
- edge_tgt: int32 [2, 16, 8, 384], P('rep', 'src', 'tgt'), may hold values from 0 to 255
- edge_count: int32 [2, 16, 8], P('rep', 'src', 'tgt'), may hold values from 192 to 384, as said below
- w_zero: float32 [640, 640], replicated, may hold values from -0.25 to 0.25
- w_one_re: float32 [512, 512], replicated, may hold values from -0.1875 to 0.1875
- w_one_im: float32 [512, 512], replicated, may hold values from -0.1875 to 0.1875
- w_two_re: float32 [384, 384], replicated, may hold values from -0.21875 to 0.21875
- w_two_im: float32 [384, 384], replicated, may hold values from -0.21875 to 0.21875
Outputs:
- grad_feats: float32 [2, 2048, 3200], P('rep', ('src', 'tgt'))
- grad_w_zero: float32 [640, 640], P('src')
- grad_w_one_re: float32 [512, 512], P('src')
- grad_w_one_im: float32 [512, 512], P('src')
- grad_w_two_re: float32 [384, 384], P('src')
- grad_w_two_im: float32 [384, 384], P('src')
Inputs may be any that keep to these rules, and one draw needn't show every extreme that they name: `edge_count`: some tile of each structure is full.
All inputs are finite; a program needn't handle non-finite values.
Results may differ from a plain program's by a relative error of at most 0.0003.
Values sent between devices are 32-bit elements; how exact they have to be, the bound alone decides.
A program may use at most 128 MiB of HBM per device.

v0:
```python
import jax
import jax.numpy as jnp
from jax import lax
from jax.sharding import PartitionSpec as P

OFFSETS = (0, 1, 10, 35, 70)
HIGH = lax.Precision.HIGHEST


def rotations(wig):
    mats = []
    for level in range(5):
        order = min(level, 2)
        rows = 2 * order + 1
        cols = 2 * level + 1
        piece = wig[OFFSETS[level] : OFFSETS[level] + rows * cols]
        mats.append(piece.reshape(rows, cols, piece.shape[-1]))
    return mats


def group(rotated, count):
    zero = jnp.stack([rotated[v][:, min(v, 2)] for v in range(5)], 1)
    plus_one = jnp.stack([rotated[v][:, min(v, 2) + 1] for v in range(1, 5)], 1)
    minus_one = jnp.stack([rotated[v][:, min(v, 2) - 1] for v in range(1, 5)], 1)
    plus_two = jnp.stack([rotated[v][:, 4] for v in range(2, 5)], 1)
    minus_two = jnp.stack([rotated[v][:, 0] for v in range(2, 5)], 1)
    return tuple((a.reshape(count, -1) for a in (zero, plus_one, minus_one, plus_two, minus_two)))


def ungroup(groups, count, chans):
    zero, plus_one, minus_one, plus_two, minus_two = [a.reshape(count, -1, chans) for a in groups]
    result = []
    for level in range(5):
        rows = []
        if level >= 2:
            rows.append(minus_two[:, level - 2])
        if level >= 1:
            rows.append(minus_one[:, level - 1])
        rows.append(zero[:, level])
        if level >= 1:
            rows.append(plus_one[:, level - 1])
        if level >= 2:
            rows.append(plus_two[:, level - 2])
        result.append(jnp.stack(rows, 1))
    return result


def tdot(left, right):
    return lax.dot_general(
        left, right, (((0,), (0,)), ((), ())), precision=HIGH, preferred_element_type=jnp.float32
    )


def ntdot(left, right):
    return lax.dot_general(
        left, right, (((1,), (1,)), ((), ())), precision=HIGH, preferred_element_type=jnp.float32
    )


def block_grads(xrows, grows, wig, weights):
    w_zero, w_one_re, w_one_im, w_two_re, w_two_im = weights
    count, coefs, chans = xrows.shape
    mats = rotations(wig)
    xrot = [
        jnp.einsum("rcb,bcf->brf", mats[v], xrows[:, v * v : (v + 1) * (v + 1)], precision=HIGH)
        for v in range(5)
    ]
    grot = [
        jnp.einsum("rcb,bcf->brf", mats[v], grows[:, v * v : (v + 1) * (v + 1)], precision=HIGH)
        for v in range(5)
    ]
    z0, zp1, zm1, zp2, zm2 = group(xrot, count)
    u0, up1, um1, up2, um2 = group(grot, count)
    grads = (
        tdot(z0, u0),
        tdot(zp1, up1) + tdot(zm1, um1),
        tdot(zp1, um1) - tdot(zm1, up1),
        tdot(zp2, up2) + tdot(zm2, um2),
        tdot(zp2, um2) - tdot(zm2, up2),
    )
    d0 = ntdot(u0, w_zero)
    dp1 = ntdot(up1, w_one_re) + ntdot(um1, w_one_im)
    dm1 = ntdot(um1, w_one_re) - ntdot(up1, w_one_im)
    dp2 = ntdot(up2, w_two_re) + ntdot(um2, w_two_im)
    dm2 = ntdot(um2, w_two_re) - ntdot(up2, w_two_im)
    back = ungroup((d0, dp1, dm1, dp2, dm2), count, chans)
    pieces = [jnp.einsum("rcb,brf->bcf", mats[v], back[v], precision=HIGH) for v in range(5)]
    return (jnp.concatenate(pieces, 1), grads)


def local(
    src_feats,
    tgt_cotangent,
    rotation,
    edge_src,
    edge_tgt,
    edge_count,
    w_zero,
    w_one_re,
    w_one_im,
    w_two_re,
    w_two_im,
):
    weights = (w_zero, w_one_re, w_one_im, w_two_re, w_two_im)
    chans = w_zero.shape[0] // 5
    feat = src_feats.shape[2]
    source_block = lax.all_gather(src_feats, "tgt", axis=1, tiled=True)[0]
    target_block = lax.all_gather(tgt_cotangent, "src", axis=1, tiled=True)[0]
    src_blk = source_block.shape[0]
    source_block = source_block.reshape(src_blk, 25, chans)
    target_block = target_block.reshape(target_block.shape[0], 25, chans)
    sources = edge_src[0, 0, 0]
    targets = edge_tgt[0, 0, 0]
    wig = rotation[0, 0, 0]
    live_count = edge_count[0, 0, 0]
    cap = sources.shape[0]
    width = 128
    atom_ids = jnp.arange(src_blk, dtype=jnp.int32)

    def step(index, carry):
        total, sums = carry
        start = index * width
        src_ids = lax.dynamic_slice_in_dim(sources, start, width)
        tgt_ids = lax.dynamic_slice_in_dim(targets, start, width)
        wig_block = lax.dynamic_slice_in_dim(wig, start, width, 1)
        live = (start + jnp.arange(width, dtype=jnp.int32) < live_count).astype(jnp.float32)
        xrows = jnp.take(source_block, src_ids, axis=0) * live[:, None, None]
        grows = jnp.take(target_block, tgt_ids, axis=0) * live[:, None, None]
        term, parts = block_grads(xrows, grows, wig_block, weights)
        onehot = (src_ids[:, None] == atom_ids[None, :]).astype(jnp.float32)
        added = tdot(onehot, term.reshape(width, feat))
        return (total + added, tuple((a + b for a, b in zip(sums, parts))))

    stop = cap // width
    init = (
        jnp.zeros((src_blk, feat), jnp.float32),
        tuple((jnp.zeros(w.shape, jnp.float32) for w in weights)),
    )
    total, sums = lax.fori_loop(0, stop, step, init)
    grad_feats = lax.psum_scatter(total[None], "tgt", scatter_dimension=1, tiled=True)
    summed = lax.psum((sums[0], sums[1], sums[2], sums[3], sums[4]), ("rep", "src", "tgt"))
    owner = lax.axis_index("src")
    parts_count = lax.axis_size("src")
    final = tuple(
        (
            lax.dynamic_slice_in_dim(
                a, owner * (a.shape[0] // parts_count), a.shape[0] // parts_count, 0
            )
            for a in summed
        )
    )
    return (grad_feats, final[0], final[1], final[2], final[3], final[4])


def solution(mesh):
    placed = (
        P("rep", ("src", "tgt"), None),
        P("rep", ("tgt", "src"), None),
        P("rep", "src", "tgt", None, None),
        P("rep", "src", "tgt", None),
        P("rep", "src", "tgt", None),
        P("rep", "src", "tgt"),
        P(),
        P(),
        P(),
        P(),
        P(),
    )
    return jax.shard_map(
        local,
        mesh=mesh,
        in_specs=placed,
        out_specs=(
            P("rep", ("src", "tgt"), None),
            P("src", None),
            P("src", None),
            P("src", None),
            P("src", None),
            P("src", None),
        ),
        check_vma=False,
    )
```

profile of v0, /device:TPU:2, one launch (start us, length us, event | category | flops | bytes accessed | tf_op | source)
XLA Modules:
  0.0 847.1 jit_solution(5621229995447299344)
XLA Ops:
  7.2 1.8 copy.146
  9.1 1.8 copy.144
  13.4 70.2 %all-gather.5.cloned.1.call-done = f32[1,128,3200]{2,0,1:T(1,128)} async-done(((f32[1,16,3200]{2,0,1:T(1,128)}), f32[1,128,3200]{2,0,1:T(1,128)}) %all-gather.5.cloned.1.call-update) | async-done | bytes 1638416 | tf_op jit(solution)/shard_map/all_gather | solution.py:107
  83.6 3.4 copy.147
  87.0 2.2 copy.149
  89.2 79.0 %all-gather.3.cloned.1.call-done = f32[1,256,3200]{2,0,1:T(1,128)} async-done(((f32[1,16,3200]{2,0,1:T(1,128)}), f32[1,256,3200]{2,0,1:T(1,128)}) %all-gather.3.cloned.1.call-update) | async-done | bytes 3276816 | tf_op jit(solution)/shard_map/all_gather | solution.py:108
  168.2 6.0 copy.145
  174.2 3.7 copy.148
  177.9 296.7 %while.24 = (s32[]{:T(128)}, f32[128,3200]{1,0:T(8,128)}, f32[640,640]{1,0:T(8,128)}, f32[512,512]{1,0:T(8,128)}, f32[512,512]{1,0:T(8,128)}, /*index=5*/f32[384...) while((s32[]{:T(128)}, f32[128,3200]{1,0:T(8,128)}, ...), condition=%wide.region_1.0_spmd.clone, body=%wide.region_0.1_spmd.clone.sunk | while | flops 6995169280 | bytes 155906560 | solution.py:139
  178.7 2.3 gather_fusion.1
  193.9 2.9 gather_fusion
  211.8 2.6 fusion.308
  223.8 2.1 fusion.304
  231.6 2.6 select_add_fusion.2
  235.4 1.9 convolution_add_fusion.8
  237.3 1.8 copy.301
  239.1 3.7 fusion.286
  244.0 1.9 convolution_subtract_fusion.7
  254.5 2.1 fusion.292
  262.8 5.7 concatenate.9
  270.3 3.8 convolution_add_fusion.10
  275.3 2.3 gather_fusion.1
  290.5 2.9 gather_fusion
  308.0 2.8 fusion.308
  320.1 3.3 fusion.304
  329.2 4.1 select_add_fusion.2
  334.5 1.9 convolution_add_fusion.8
  336.4 1.8 copy.301
  338.2 3.7 fusion.286
  343.2 1.9 convolution_subtract_fusion.7
  353.6 2.2 fusion.292
  358.7 1.8 fusion.290
  362.1 5.7 concatenate.9
  369.6 4.3 convolution_add_fusion.10
  374.9 2.3 gather_fusion.1
  390.1 2.9 gather_fusion
  407.6 2.8 fusion.308
  419.8 3.3 fusion.304
  428.9 4.1 select_add_fusion.2
  434.2 1.9 convolution_add_fusion.8
  436.1 1.8 copy.301
  438.0 3.7 fusion.286
  442.9 1.9 convolution_subtract_fusion.7
  453.4 2.0 fusion.292
  461.6 5.7 concatenate.9
  469.1 4.3 convolution_add_fusion.10
  475.2 271.2 %all-reduce.3.cloned.1.call-done = (f32[640,640]{1,0:T(8,128)}, f32[512,512]{1,0:T(8,128)}, f32[512,512]{1,0:T(8,128)}, f32[384,384]{1,0:T(8,128)}, f32[384,384]{1,0:T(8,128)}) async-done(((f32[640,640]{1,0:T(8,128)}, f32[512,512]{1,0:T(8,128)}, f32[512,512]{1,0:T(8,128)}, f32[384,384]{1,0:T(8,128)}, f32[384,384]{1,0:T(8,128)}), (f32[640,640]{1,0:T(8,128)}, f32[512,512]{1,0:T(8,128)}, f32[512,512]{1,0:T(8,128)}, ...) | async-done | bytes 4915216 | tf_op jit(solution)/shard_map/psum | solution.py:141
  750.9 89.4 %reduce-scatter.2.cloned.1.call-done = f32[1,16,3200]{2,1,0:T(8,128)} async-done(((f32[1,128,3200]{2,1,0:T(8,128)}), f32[1,16,3200]{2,1,0:T(8,128)}) %reduce-scatter.2.cloned.1.call-update) | async-done | bytes 204816 | tf_op jit(solution)/shard_map/reduce_scatter | solution.py:140
  (649 shorter events, 190.4 us)
Async XLA Ops:
  7.2 76.4 %all-gather.5.cloned.1.call-start = ((), (), s32[]{:S(2)}) async-start(), calls=%async_computation.2 | async-start | bytes 1843200 | tf_op jit(solution)/shard_map/all_gather | solution.py:107
  9.1 159.1 %all-gather.3.cloned.1.call-start = ((), (), s32[]{:S(2)}) async-start(), calls=%async_computation.1 | async-start | bytes 3481600 | tf_op jit(solution)/shard_map/all_gather | solution.py:108
  11.0 735.5 %all-reduce.3.cloned.1.call-start = ((), (), s32[]{:S(2)}) async-start(), calls=%async_computation.4 | async-start | bytes 9830400 | tf_op jit(solution)/shard_map/psum | solution.py:141
  177.9 5.5 copy-start.48
  177.9 15.9 %copy-start.52 = (s32[384]{0:T(512)}, s32[384]{0:T(512)S(1)}, u32[]{:S(2)}) copy-start(s32[384]{0:T(512)S(1)} %get-tuple-element.817) | copy-start | bytes 4612 | tf_op jit(solution)/shard_map/while
  183.7 3.9 slice-start
  187.6 3.8 copy-start.2
  187.7 3.8 slice-start.1
  215.1 3.8 copy-start.34
  217.7 4.2 copy-start.38
  217.7 4.2 copy-start.40
  217.7 4.2 copy-start.41
  244.0 3.8 copy-start.9
  270.3 3.8 copy-start.49
  270.3 3.8 copy-start.51
  270.3 3.8 copy-start.53
  274.5 5.5 copy-start.48
  274.5 15.9 %copy-start.52 = (s32[384]{0:T(512)}, s32[384]{0:T(512)S(1)}, u32[]{:S(2)}) copy-start(s32[384]{0:T(512)S(1)} %get-tuple-element.817) | copy-start | bytes 4612 | tf_op jit(solution)/shard_map/while
  280.3 3.9 slice-start
  284.3 3.8 copy-start.2
  284.3 3.8 slice-start.1
  308.0 3.5 copy-start.15
  311.5 3.8 copy-start.34
  314.1 4.2 copy-start.38
  314.1 4.2 copy-start.40
  314.1 4.2 copy-start.41
  329.1 4.1 copy-start.7
  343.1 3.8 copy-start.9
  369.6 4.3 copy-start.49
  369.6 4.3 copy-start.51
  369.6 4.3 copy-start.53
  374.1 5.5 copy-start.48
  374.1 15.9 %copy-start.52 = (s32[384]{0:T(512)}, s32[384]{0:T(512)S(1)}, u32[]{:S(2)}) copy-start(s32[384]{0:T(512)S(1)} %get-tuple-element.817) | copy-start | bytes 4612 | tf_op jit(solution)/shard_map/while
  379.9 3.9 slice-start
  383.8 3.8 copy-start.2
  383.8 3.8 slice-start.1
  401.4 3.4 copy-start.23
  407.6 3.5 copy-start.15
  411.1 3.8 copy-start.34
  413.7 4.2 copy-start.38
  413.7 4.2 copy-start.40
  413.7 4.2 copy-start.41
  428.9 4.1 copy-start.7
  442.9 3.8 copy-start.9
  469.1 4.3 copy-start.49
  469.1 4.3 copy-start.51
  469.1 4.3 copy-start.53
  474.6 365.7 %reduce-scatter.2.cloned.1.call-start = ((), (), s32[]{:S(2)}) async-start(), calls=%async_computation.3 | async-start | bytes 1843200 | tf_op jit(solution)/shard_map/reduce_scatter | solution.py:140
  (127 other events, 261.1 us)
Sparse Core Ops, SparseCore 0:
  10.6 72.9 all-gather.4
  86.0 82.1 all-gather.2
  474.7 271.6 all-reduce.2
  750.9 89.3 reduce-scatter.1
where the time goes:
time: 852 us; the launch traced here: 847 us
  waiting for transfers between devices  510 us (60%)
  local copies, waits for them, and re-layouts  145 us (17%)
  matrix products  144 us (17%)
  other arithmetic  28.3 us (3%)
  between operations  14.1 us (2%)
    psum x1, waiting for transfers between devices, local(): lax.psum((sums[0], sums[1], sums[2], sums[3], sums[4]), ('rep', 'src', 't...  271 us
    reduce_scatter x1, waiting for transfers between devices, local(): lax.psum_scatter(total[None], 'tgt', scatter_dimension=1, tiled=True)  89.4 us
    all_gather x1, waiting for transfers between devices, local(): target_block = lax.all_gather(tgt_cotangent, 'src', axis=1, tiled=True)[0]  79 us
    all_gather x1, waiting for transfers between devices, local(): source_block = lax.all_gather(src_feats, 'tgt', axis=1, tiled=True)[0]  70.2 us
    dot_general x30, matrix products, tdot(): lax.dot_general(left, right, (((0,), (0,)), ((), ())), precision=HIGH, pr...  58.3 us
    dot_general x27, matrix products, ntdot(): lax.dot_general(left, right, (((1,), (1,)), ((), ())), precision=HIGH, pr...  39.2 us
    while x357, local copies, waits for them, and re-layouts  25.1 us
    concatenate x6, local copies, waits for them, and re-layouts, block_grads(): return (jnp.concatenate(pieces, 1), grads)  22.6 us
  transfers between devices with their start and end apart: 4, of which 4 were waited for; matrix products, arithmetic and copies ran while one was open for 2% of the time, Pallas kernels for 0%

commit v1 on v0

--- a/solution.py
+++ b/solution.py
@@ -138,7 +138,9 @@
     )
     total, sums = lax.fori_loop(0, stop, step, init)
     grad_feats = lax.psum_scatter(total[None], "tgt", scatter_dimension=1, tiled=True)
-    summed = lax.psum((sums[0], sums[1], sums[2], sums[3], sums[4]), ("rep", "src", "tgt"))
+    summed = (sums[0], sums[1], sums[2], sums[3], sums[4])
+    for name in ("rep", ("src", "tgt")):
+        summed = lax.psum(summed, name)
     owner = lax.axis_index("src")
     parts_count = lax.axis_size("src")
     final = tuple(

time: 852 us -> 866 us (1.016)
  waiting for transfers between devices: 510 us -> 524 us
    psum x1 -> x2, waiting for transfers between devices: 271 us -> 285 us  [local(): summed = lax.psum(summed, name)]
  transfers between devices with their start and end apart: 4 -> 5, of which waited for: 4 -> 5; matrix products, arithmetic and copies ran while one was open for 2% -> 2% of each run, Pallas kernels for 0% -> 0%
where the time goes in v1:
time: 866 us; the launch traced here: 861 us
  waiting for transfers between devices  524 us (61%)
  local copies, waits for them, and re-layouts  145 us (17%)
  matrix products  144 us (17%)
  other arithmetic  28.3 us (3%)
  between operations  14.1 us (2%)
    psum x2, waiting for transfers between devices, local(): summed = lax.psum(summed, name)  285 us
    reduce_scatter x1, waiting for transfers between devices, local(): lax.psum_scatter(total[None], 'tgt', scatter_dimension=1, tiled=True)  89.5 us
    all_gather x1, waiting for transfers between devices, local(): target_block = lax.all_gather(tgt_cotangent, 'src', axis=1, tiled=True)[0]  79 us
    all_gather x1, waiting for transfers between devices, local(): source_block = lax.all_gather(src_feats, 'tgt', axis=1, tiled=True)[0]  70.2 us
    dot_general x30, matrix products, tdot(): lax.dot_general(left, right, (((0,), (0,)), ((), ())), precision=HIGH, pr...  58.3 us
    dot_general x27, matrix products, ntdot(): lax.dot_general(left, right, (((1,), (1,)), ((), ())), precision=HIGH, pr...  39.2 us
    while x357, local copies, waits for them, and re-layouts  25.1 us
    concatenate x6, local copies, waits for them, and re-layouts, block_grads(): return (jnp.concatenate(pieces, 1), grads)  22.6 us
  transfers between devices with their start and end apart: 5, of which 5 were waited for; matrix products, arithmetic and copies ran while one was open for 2% of the time, Pallas kernels for 0%

profile of v1, /device:TPU:2, one launch (start us, length us, event | category | flops | bytes accessed | tf_op | source)
XLA Modules:
  0.0 861.2 jit_solution(5275825503685481522)
XLA Ops:
  7.2 1.8 copy.146
  9.1 1.8 copy.144
  13.4 70.2 %all-gather.5.cloned.1.call-done = f32[1,128,3200]{2,0,1:T(1,128)} async-done(((f32[1,16,3200]{2,0,1:T(1,128)}), f32[1,128,3200]{2,0,1:T(1,128)}) %all-gather.5.cloned.1.call-update) | async-done | bytes 1638416 | tf_op jit(solution)/shard_map/all_gather | solution.py:107
  83.6 3.4 copy.147
  87.0 2.2 copy.149
  89.2 79.0 %all-gather.3.cloned.1.call-done = f32[1,256,3200]{2,0,1:T(1,128)} async-done(((f32[1,16,3200]{2,0,1:T(1,128)}), f32[1,256,3200]{2,0,1:T(1,128)}) %all-gather.3.cloned.1.call-update) | async-done | bytes 3276816 | tf_op jit(solution)/shard_map/all_gather | solution.py:108
  168.2 6.0 copy.145
  174.2 3.7 copy.148
  177.9 296.6 %while.24 = (s32[]{:T(128)}, f32[128,3200]{1,0:T(8,128)}, f32[640,640]{1,0:T(8,128)}, f32[512,512]{1,0:T(8,128)}, f32[512,512]{1,0:T(8,128)}, /*index=5*/f32[384...) while((s32[]{:T(128)}, f32[128,3200]{1,0:T(8,128)}, ...), condition=%wide.region_1.0_spmd.clone, body=%wide.region_0.1_spmd.clone.sunk | while | flops 6995169280 | bytes 155906560 | solution.py:139
  178.7 2.3 gather_fusion.1
  193.9 2.9 gather_fusion
  211.8 2.6 fusion.308
  223.8 2.1 fusion.304
  231.6 2.6 select_add_fusion.2
  235.4 1.9 convolution_add_fusion.8
  237.3 1.8 copy.301
  239.1 3.7 fusion.286
  244.0 1.9 convolution_subtract_fusion.7
  254.5 2.1 fusion.292
  262.7 5.7 concatenate.9
  270.3 3.8 convolution_add_fusion.10
  275.3 2.3 gather_fusion.1
  290.5 2.9 gather_fusion
  308.0 2.8 fusion.308
  320.1 3.3 fusion.304
  329.1 4.1 select_add_fusion.2
  334.5 1.9 convolution_add_fusion.8
  336.3 1.8 copy.301
  338.2 3.7 fusion.286
  343.1 1.9 convolution_subtract_fusion.7
  353.5 2.2 fusion.292
  362.0 5.7 concatenate.9
  369.5 4.3 convolution_add_fusion.10
  374.8 2.3 gather_fusion.1
  390.0 2.9 gather_fusion
  407.6 2.8 fusion.308
  419.7 3.3 fusion.304
  428.8 4.1 select_add_fusion.2
  434.1 1.9 convolution_add_fusion.8
  436.0 1.8 copy.301
  437.9 3.7 fusion.286
  442.8 1.9 convolution_subtract_fusion.7
  453.2 2.0 fusion.292
  461.4 5.7 concatenate.9
  469.0 4.3 convolution_add_fusion.10
  474.6 39.4 %all-reduce.7.cloned.1.call-done = (f32[640,640]{1,0:T(8,128)}, f32[512,512]{1,0:T(8,128)}, f32[512,512]{1,0:T(8,128)}, f32[384,384]{1,0:T(8,128)}, f32[384,384]{1,0:T(8,128)}) async-done(((f32[640,640]{1,0:T(8,128)}, f32[512,512]{1,0:T(8,128)}, f32[512,512]{1,0:T(8,128)}, f32[384,384]{1,0:T(8,128)}, f32[384,384]{1,0:T(8,128)}), (f32[640,640]{1,0:T(8,128)}, f32[512,512]{1,0:T(8,128)}, f32[512,512]{1,0:T(8,128)}, ...) | async-done | bytes 4915216 | tf_op jit(solution)/shard_map/psum | solution.py:143
  514.6 245.8 %all-reduce.5.cloned.1.call-done = (f32[640,640]{1,0:T(8,128)}, f32[512,512]{1,0:T(8,128)}, f32[512,512]{1,0:T(8,128)}, f32[384,384]{1,0:T(8,128)}, f32[384,384]{1,0:T(8,128)}) async-done(((f32[640,640]{1,0:T(8,128)}, f32[512,512]{1,0:T(8,128)}, f32[512,512]{1,0:T(8,128)}, f32[384,384]{1,0:T(8,128)}, f32[384,384]{1,0:T(8,128)}), (f32[640,640]{1,0:T(8,128)}, f32[512,512]{1,0:T(8,128)}, f32[512,512]{1,0:T(8,128)}, ...) | async-done | bytes 4915216 | tf_op jit(solution)/shard_map/psum | solution.py:143
  764.9 89.5 %reduce-scatter.2.cloned.1.call-done = f32[1,16,3200]{2,1,0:T(8,128)} async-done(((f32[1,128,3200]{2,1,0:T(8,128)}), f32[1,16,3200]{2,1,0:T(8,128)}) %reduce-scatter.2.cloned.1.call-update) | async-done | bytes 204816 | tf_op jit(solution)/shard_map/reduce_scatter | solution.py:140
  (652 shorter events, 192.3 us)
Async XLA Ops:
  7.2 76.4 %all-gather.5.cloned.1.call-start = ((), (), s32[]{:S(2)}) async-start(), calls=%async_computation.2 | async-start | bytes 1843200 | tf_op jit(solution)/shard_map/all_gather | solution.py:107
  9.1 159.1 %all-gather.3.cloned.1.call-start = ((), (), s32[]{:S(2)}) async-start(), calls=%async_computation.1 | async-start | bytes 3481600 | tf_op jit(solution)/shard_map/all_gather | solution.py:108
  10.9 503.0 %all-reduce.7.cloned.1.call-start = ((), (), s32[]{:S(2)}) async-start(), calls=%async_computation.5 | async-start | bytes 9830400 | tf_op jit(solution)/shard_map/psum | solution.py:143
  177.9 5.5 copy-start.48
  177.9 15.9 %copy-start.52 = (s32[384]{0:T(512)}, s32[384]{0:T(512)S(1)}, u32[]{:S(2)}) copy-start(s32[384]{0:T(512)S(1)} %get-tuple-element.822) | copy-start | bytes 4612 | tf_op jit(solution)/shard_map/while
  183.7 3.9 slice-start
  187.6 3.8 copy-start.2
  187.6 3.8 slice-start.1
  215.1 3.8 copy-start.34
  217.7 4.2 copy-start.38
  217.7 4.2 copy-start.40
  217.7 4.2 copy-start.41
  244.0 3.8 copy-start.9
  270.2 3.8 copy-start.49
  270.2 3.8 copy-start.51
  270.3 3.8 copy-start.53
  274.5 5.5 copy-start.48
  274.5 15.9 %copy-start.52 = (s32[384]{0:T(512)}, s32[384]{0:T(512)S(1)}, u32[]{:S(2)}) copy-start(s32[384]{0:T(512)S(1)} %get-tuple-element.822) | copy-start | bytes 4612 | tf_op jit(solution)/shard_map/while
  280.3 3.9 slice-start
  284.2 3.8 copy-start.2
  284.2 3.8 slice-start.1
  308.0 3.5 copy-start.15
  311.5 3.8 copy-start.34
  314.0 4.2 copy-start.38
  314.1 4.2 copy-start.40
  314.1 4.2 copy-start.41
  329.1 4.1 copy-start.7
  343.1 3.8 copy-start.9
  369.5 4.3 copy-start.49
  369.5 4.3 copy-start.51
  369.5 4.3 copy-start.53
  374.0 5.5 copy-start.48
  374.0 15.9 %copy-start.52 = (s32[384]{0:T(512)}, s32[384]{0:T(512)S(1)}, u32[]{:S(2)}) copy-start(s32[384]{0:T(512)S(1)} %get-tuple-element.822) | copy-start | bytes 4612 | tf_op jit(solution)/shard_map/while
  379.8 3.9 slice-start
  383.7 3.8 copy-start.2
  383.7 3.8 slice-start.1
  407.6 3.5 copy-start.15
  411.0 3.8 copy-start.34
  413.6 4.2 copy-start.38
  413.6 4.2 copy-start.40
  413.6 4.2 copy-start.41
  428.8 4.1 copy-start.7
  442.8 3.8 copy-start.9
  469.0 4.3 copy-start.49
  469.0 4.3 copy-start.51
  469.0 4.3 copy-start.53
  474.5 285.9 %all-reduce.5.cloned.1.call-start = ((), (), s32[]{:S(2)}) async-start(), calls=%async_computation.4 | async-start | bytes 9830400 | tf_op jit(solution)/shard_map/psum | solution.py:143
  514.0 340.4 %reduce-scatter.2.cloned.1.call-start = ((), (), s32[]{:S(2)}) async-start(), calls=%async_computation.3 | async-start | bytes 1843200 | tf_op jit(solution)/shard_map/reduce_scatter | solution.py:140
  (128 other events, 264.3 us)
Sparse Core Ops, SparseCore 0:
  10.6 72.9 all-gather.4
  86.0 82.1 all-gather.2
  474.6 39.3 all-reduce.6
  520.2 240.1 all-reduce.4
  765.5 88.8 reduce-scatter.1
